TPU v7x, 512 devices: a whole 4x4x16 slice. The times are simulated.
512 devices in a mesh: mom: 32 (over z, core), hist: 16 (over y, x).
Axes of the slice: x: 4, y: 4, z: 16, core: 2. Of those that a mesh axis runs over, the one named last changes fastest.
Arguments:
- green_hist: float32 [2, 2, 2, 4096, 4096], P(None, None, None, 'mom', 'hist'), may hold values from 0.5 to 1.5
- sigma_row: float32 [2, 2, 2, 4096], P(None, None, None, 'hist'), may hold values from -6 to 6
- coupling_row: float32 [2, 2, 2, 4096], P(None, None, None, 'hist'), may hold values from -3 to 3
- prop_prev: float32 [2, 2, 2, 4096], P(None, None, None, 'mom'), may hold values from 0.5 to 1.5
- init_state: float32 [4], replicated, may hold values from 0.5 to 1.5
- state_rates: float32 [4], replicated, may hold values from 0.05 to 2
- source_row: float32 [4, 4096], P(None, 'hist'), may hold values from -6 to 6
- mom_ids: int32 [4096], P('mom'), may hold values from 0 to 4095, each once
- t_step: int32 [1], replicated, may hold values from 0 to 2999
- block_len: int32 [16], replicated, may hold values from 1 to 256, 2560 in all
Outputs:
- prop_new: float32 [2, 2, 2, 4096], P(None, None, None, 'mom')
- pp_row: float32 [4, 4096], P(None, 'hist')
- hyb_row: float32 [2, 2, 2, 4096], P(None, None, None, 'hist')
Inputs may be any that keep to these rules, and one draw needn't show every extreme that they name: `mom_ids`: each momentum point 0 .. 4095 appears once. `block_len`: the entries sum to 2560; the largest is 256.
All inputs are finite; a program needn't handle non-finite values.
Results may differ from a plain program's by a relative error of at most 0.00035.
Values sent between devices are 32-bit elements; how exact they have to be, the bound alone decides.
A program may use at most 64 MiB of HBM per device.

v0:
```python
import math

import jax
import jax.numpy as jnp
import numpy as np
from jax import lax
from jax.sharding import PartitionSpec as P

LK = 64


TIME_STEP = 0.005
HOPPING_TIME = 0.5
FIELD_STEP = 0.0025


def entering(value, axis, join, neutral):
    count, mine = (lax.axis_size(axis), lax.axis_index(axis))
    pieces = jax.tree.map(lambda part: lax.all_gather(part, axis), value)
    so_far = jax.tree.map(
        lambda part, zero: jnp.full_like(part, 0) + jnp.asarray(zero, part.dtype), value, neutral
    )

    def step(position, so_far):
        longer = join(so_far, jax.tree.map(lambda part: part[position], pieces))
        return jax.tree.map(lambda new, old: jnp.where(position < mine, new, old), longer, so_far)

    return lax.fori_loop(0, count - 1, step, so_far)


def from_root(value, axis, source):
    kept = jnp.where(lax.axis_index(axis) == source, value, 0).astype(value.dtype)
    return lax.psum(kept, axis)


def parity_sign(value):
    sign_value = 1
    for position in range(4):
        if value >> position & 1:
            sign_value = -sign_value
    return sign_value


def fock_table():
    table = np.zeros((2, 2, 4, 4), np.float32)
    for state_in in range(4):
        for orb_b in range(2):
            if state_in >> orb_b & 1:
                sign_b = parity_sign(state_in & (1 << orb_b) - 1)
                middle = state_in ^ 1 << orb_b
                for orb_a in range(2):
                    if not middle >> orb_a & 1:
                        sign_a = parity_sign(middle & (1 << orb_a) - 1)
                        state_out = middle | 1 << orb_a
                        table[orb_a, orb_b, state_out, state_in] += sign_a * sign_b
    return jnp.asarray(table, jnp.float32)


def complex_product(left, right):
    hp = lax.Precision.HIGHEST
    real_part = jnp.einsum("ab...,bc...->ac...", left[0], right[0], precision=hp) - jnp.einsum(
        "ab...,bc...->ac...", left[1], right[1], precision=hp
    )
    imag_part = jnp.einsum("ab...,bc...->ac...", left[0], right[1], precision=hp) + jnp.einsum(
        "ab...,bc...->ac...", left[1], right[0], precision=hp
    )
    return jnp.stack([real_part, imag_part])


def memory_sum(weighted, history):
    hp = lax.Precision.HIGHEST
    real_part = jnp.einsum("abs,bcks->ack", weighted[0], history[0], precision=hp) - jnp.einsum(
        "abs,bcks->ack", weighted[1], history[1], precision=hp
    )
    imag_part = jnp.einsum("abs,bcks->ack", weighted[0], history[1], precision=hp) + jnp.einsum(
        "abs,bcks->ack", weighted[1], history[0], precision=hp
    )
    return jnp.stack([real_part, imag_part])


def row_product(current, history):
    hp = lax.Precision.HIGHEST
    real_part = jnp.einsum("ack,bcks->abs", current[0], history[0], precision=hp) + jnp.einsum(
        "ack,bcks->abs", current[1], history[1], precision=hp
    )
    imag_part = jnp.einsum("ack,bcks->abs", current[1], history[0], precision=hp) - jnp.einsum(
        "ack,bcks->abs", current[0], history[1], precision=hp
    )
    return jnp.stack([real_part, imag_part])


def momentum_phase(mom_ids, t_step, total):
    field = FIELD_STEP * t_step[0].astype(jnp.float32)
    along_x = 2.0 * math.pi * (mom_ids % LK).astype(jnp.float32) / LK
    along_y = 2.0 * math.pi * (mom_ids // LK).astype(jnp.float32) / (total // LK)
    energy = -2.0 * (jnp.cos(along_x - field) + jnp.cos(along_y - field))
    angle = HOPPING_TIME * energy
    return (jnp.cos(angle), jnp.sin(angle))


def advance(previous, memory, cosine, sine):
    summed = previous + memory
    real_part = cosine * summed[0] + sine * summed[1]
    imag_part = cosine * summed[1] - sine * summed[0]
    return jnp.stack([real_part, imag_part])


def compose(earlier, later):
    hp = lax.Precision.HIGHEST
    mats = jnp.einsum("...nm,...mk->...nk", later[0], earlier[0], precision=hp)
    vecs = jnp.einsum("...nm,...m->...n", later[0], earlier[1], precision=hp) + later[1]
    return (mats, vecs)


def on_device(
    green_hist,
    sigma_row,
    coupling_row,
    prop_prev,
    init_state,
    state_rates,
    source_row,
    mom_ids,
    t_step,
    block_len,
):
    slots_dev = green_hist.shape[-1]
    mom_dev = green_hist.shape[3]
    mom_count = lax.axis_size("mom")
    hist_count = lax.axis_size("hist")
    total = mom_dev * mom_count
    hist_pos = lax.axis_index("hist")
    length = lax.dynamic_slice_in_dim(block_len, hist_pos, 1, 0)[0]
    live_mask = jnp.arange(slots_dev, dtype=jnp.int32) < length
    weight = jnp.where(live_mask, jnp.float32(TIME_STEP), jnp.float32(0.0))
    memory_part = memory_sum(sigma_row * weight, green_hist)
    cosine, sine = momentum_phase(mom_ids, t_step, total)
    memory = lax.psum(memory_part, "hist")
    prop_new = advance(prop_prev, memory, cosine, sine)
    row_part = row_product(prop_new, green_hist) / total
    row_part = jnp.where(live_mask, row_part, jnp.float32(0.0))
    local_row = lax.psum(row_part, "mom")
    delta = complex_product(local_row, coupling_row)
    table = fock_table()
    lam = jnp.einsum("abs,abnm->snm", delta[0], table, precision=lax.Precision.HIGHEST)
    retain = jnp.diag(jnp.exp(-state_rates / (slots_dev * hist_count)))
    identity = jnp.eye(init_state.shape[0], dtype=jnp.float32)
    mats = jnp.where(live_mask[:, None, None], retain[None] - TIME_STEP * lam, identity[None])
    vecs = jnp.where(live_mask[:, None], TIME_STEP * source_row.T, jnp.float32(0.0))
    cum_mats, cum_vecs = lax.associative_scan(compose, (mats, vecs), axis=0)
    block_map = (cum_mats[-1], cum_vecs[-1])
    prior = entering(block_map, "hist", compose, (identity, jnp.zeros_like(init_state)))
    start_state = jnp.dot(prior[0], init_state, precision=lax.Precision.HIGHEST) + prior[1]
    states = (
        jnp.einsum("snm,m->sn", cum_mats, start_state, precision=lax.Precision.HIGHEST) + cum_vecs
    )
    final_state = from_root(states[-1], "hist", hist_count - 1)
    pp_row = states.T
    scale = 1.0 / jnp.sqrt(1.0 + jnp.sum(final_state * final_state))
    hyb_row = delta * scale
    return (prop_new, pp_row, hyb_row)


def solution(mesh):
    placed = (
        P(None, None, None, "mom", "hist"),
        P(None, None, None, "hist"),
        P(None, None, None, "hist"),
        P(None, None, None, "mom"),
        P(),
        P(),
        P(None, "hist"),
        P("mom"),
        P(),
        P(),
    )
    return jax.shard_map(
        on_device,
        mesh=mesh,
        in_specs=placed,
        out_specs=(P(None, None, None, "mom"), P(None, "hist"), P(None, None, None, "hist")),
        check_vma=False,
    )
```

profile of v0, /device:TPU:2, one launch (start us, length us, event | category | flops | bytes accessed | tf_op | source)
XLA Modules:
  0.0 226.2 jit_solution(4658161577168113196)
XLA Ops:
  1.3 0.6 copy-done.15
  2.5 0.6 iota_compare_fusion.1
  3.2 0.7 broadcast_select_fusion.2
  3.9 0.6 copy-done.14
  6.1 0.7 copy-done.11
  7.1 1.3 fusion.111
  10.6 41.4 %psum.21 = f32[2,2,2,128]{3,1,2,0:T(2,128)S(1)} all-reduce(f32[2,2,2,128]{3,1,2,0:T(2,128)S(1)} %pad_maximum_fusion.6), channel_id=1, replica_groups=mesh['mom'=32,'hist'=16] {'hist'}, use_global_device_ids=true, to_apply=%region_0.1 | all-reduce | flops 1024 | bytes 8192 | tf_op jit(solution)/shard_map/psum | solution.py:138
  52.7 0.6 copy.173
  54.0 48.5 %psum.22 = f32[2,2,2,256]{3,1,2,0:T(2,128)S(1)} all-reduce(f32[2,2,2,256]{3,1,2,0:T(2,128)S(1)} %fusion.70), channel_id=1, replica_groups=mesh['mom'=32,'hist'=16] {'mom'}, use_global_device_ids=true, to_apply=%region_1.2 | all-reduce | flops 2048 | bytes 16384 | tf_op jit(solution)/shard_map/psum | solution.py:142
  102.9 1.8 fusion.28
  104.7 1.8 fusion.32
  106.5 1.9 convolution_subtract_fusion
  108.4 1.9 fusion.11
  113.6 1.0 fusion.113
  120.8 0.7 slice-done.5
  122.3 0.7 slice-done.4
  123.9 0.6 slice-done.3
  125.6 0.6 slice-done.2
  127.7 0.6 slice-done.1
  129.0 0.7 slice-done.6
  130.4 21.8 %all-gather = f32[16,1,4]{2,1,0:T(1,128)S(1)} all-gather(f32[1,1,4]{2,1,0:T(1,128)S(1)} %bitcast.255), channel_id=1, replica_groups=mesh['mom'=32,'hist'=16] {'hist'}, dimensions={0}, use_global_device_ids=true | all-gather | bytes 272 | tf_op jit(solution)/shard_map/all_gather | solution.py:19
  153.6 0.6 slice-done
  154.2 0.8 pad.110
  155.1 0.8 pad.111
  156.1 1.0 fusion.34
  157.2 1.7 pad.112
  158.9 1.7 pad.113
  160.5 21.1 %all_gather.6 = f32[16,4,4]{2,1,0:T(4,128)S(1)} all-gather(f32[1,4,4]{2,1,0:T(4,128)S(1)} %slice_add_fusion), channel_id=1, replica_groups=mesh['mom'=32,'hist'=16] {'hist'}, dimensions={0}, use_global_device_ids=true | all-gather | bytes 1088 | tf_op jit(solution)/shard_map/all_gather | solution.py:19
  181.7 4.4 %while.16 = (s32[]{:T(128)}, f32[4,4]{1,0:T(4,128)S(1)}, f32[4]{0:T(128)S(1)}, s32[]{:T(128)}, f32[16,4,4]{2,1,0:T(4,128)S(1)}, /*index=5*/f32[16,4]{1,0:T(8,128)S(1)}, s32[]{:T(128)}, s32[]{:T(128)}) while((s32[]{:T(128)}, f32[4,4]{1,0:T(4,128)S(1)}, f32[4]{0:T(128)S(1)}, s32[]{:T(128)}, f32[16,4,4]{2,1,0:T(4,128)S(1)}, ...), condition=%wide.region_3.4_spmd.clone, body=%wide.region_2.3_spmd.clone.sunk | while | flops 996 | bytes 12644 | solution.py:28
  186.9 37.5 %psum.23 = f32[4]{0:T(128)S(1)} all-reduce(f32[4]{0:T(128)S(1)} %fusion.86), channel_id=1, replica_groups=mesh['mom'=32,'hist'=16] {'hist'}, use_global_device_ids=true, to_apply=%region_4.5 | all-reduce | flops 4 | bytes 32 | tf_op jit(solution)/shard_map/psum | solution.py:33
  224.3 0.6 multiply_reduce_fusion.14
  225.6 0.6 maximum_multiply_fusion.1
  (285 shorter events, 28.1 us)
Async XLA Ops:
  0.6 185.4 %copy-start = (f32[4]{0:T(128)S(1)}, f32[4]{0:T(128)}, u32[]{:S(2)}) copy-start(f32[4]{0:T(128)} %param.17) | copy-start | bytes 52
  1.3 0.7 copy-start.15
  3.2 0.7 copy-start.16
  3.9 0.7 copy-start.14
  4.7 0.7 copy-start.13
  5.4 0.7 copy-start.8
  5.4 0.7 copy-start.10
  6.1 0.7 copy-start.11
  8.4 43.5 %copy-start.1 = (f32[2,2,2,128,256]{4,3,2,1,0:T(8,128)S(1)}, f32[2,2,2,128,256]{4,3,2,1,0:T(8,128)}, u32[]{:S(2)}) copy-start(f32[2,2,2,128,256]{4,3,2,1,0:T(8,128)} %param.13) | copy-start | bytes 3145732
  10.5 41.4 %copy-start.12 = (f32[2,2,2,128]{3,2,1,0:T(2,128)S(1)}, f32[2,2,2,128]{3,2,1,0:T(2,128)}, u32[]{:S(2)}) copy-start(f32[2,2,2,128]{3,2,1,0:T(2,128)} %param.16) | copy-start | bytes 12292
  110.5 0.7 copy-start.17
  114.5 38.4 %copy-start.2 = (f32[128,4,4]{2,1,0:T(4,128)}, f32[128,4,4]{2,1,0:T(4,128)S(1)}, u32[]{:S(2)}) copy-start(f32[128,4,4]{2,1,0:T(4,128)S(1)} %fusion.113) | copy-start | bytes 24580
  115.8 11.5 %copy-start.3 = (f32[64,4,4]{2,1,0:T(4,128)}, f32[64,4,4]{2,1,0:T(4,128)S(1)}, u32[]{:S(2)}) copy-start(f32[64,4,4]{2,1,0:T(4,128)S(1)} %fusion.38) | copy-start | bytes 12292
  116.8 8.5 %copy-start.4 = (f32[32,4,4]{2,1,0:T(4,128)}, f32[32,4,4]{2,1,0:T(4,128)S(1)}, u32[]{:S(2)}) copy-start(f32[32,4,4]{2,1,0:T(4,128)S(1)} %fusion.46) | copy-start | bytes 6148
  117.7 6.0 %copy-start.5 = (f32[16,4,4]{2,1,0:T(4,128)}, f32[16,4,4]{2,1,0:T(4,128)S(1)}, u32[]{:S(2)}) copy-start(f32[16,4,4]{2,1,0:T(4,128)S(1)} %fusion.54) | copy-start | bytes 3076
  118.4 3.7 %copy-start.6 = (f32[8,4,4]{2,1,0:T(4,128)}, f32[8,4,4]{2,1,0:T(4,128)S(1)}, u32[]{:S(2)}) copy-start(f32[8,4,4]{2,1,0:T(4,128)S(1)} %fusion.62) | copy-start | bytes 1540
  119.1 1.5 copy-start.7
  120.7 0.7 slice-start.5
  122.3 0.7 slice-start.4
  123.8 0.7 slice-start.3
  125.6 0.7 slice-start.2
  127.7 0.7 slice-start.1
  129.0 0.7 slice-start.6
  153.5 0.7 slice-start
  186.7 38.9 %copy-start.9 = (f32[256,4]{0,1:T(4,128)}, f32[256,4]{0,1:T(4,128)S(1)}, u32[]{:S(2)}) copy-start(f32[256,4]{0,1:T(4,128)S(1)} %add_add_fusion) | copy-start | bytes 12292
where the time goes:
time: 227 us; the launch traced here: 226 us
  blocking collectives  170 us (75%)
  local copies, waits for them, and re-layouts  26.3 us (12%)
  matrix products  21.2 us (9%)
  other arithmetic  5.78 us (3%)
  between operations  2.72 us (1%)
    psum x1, blocking collectives, on_device(): local_row = lax.psum(row_part, 'mom')  48.5 us
    all_gather x2, blocking collectives, entering(): pieces = jax.tree.map(lambda part: lax.all_gather(part, axis), value)  42.9 us
    psum x1, blocking collectives, on_device(): memory = lax.psum(memory_part, 'hist')  41.4 us
    psum x1, blocking collectives, from_root(): return lax.psum(kept, axis)  37.5 us
    slice x45, local copies, waits for them, and re-layouts, on_device(): cum_mats, cum_vecs = lax.associative_scan(compose, (mats, vecs), axis=0)  9.1 us
    pad x28, local copies, waits for them, and re-layouts, on_device(): cum_mats, cum_vecs = lax.associative_scan(compose, (mats, vecs), axis=0)  8.22 us
    dot_general x30, matrix products, compose(): mats = jnp.einsum('...nm,...mk->...nk', later[0], earlier[0], precision=hp)  7.39 us
    unnamed x50, local copies, waits for them, and re-layouts  5.18 us

commit v1 on v0

v1 whole, which is shorter than its diff:
```python
import functools
import math

import jax
import jax.numpy as jnp
import numpy as np
from jax import lax
from jax.experimental import pallas as pl
from jax.experimental.pallas import tpu as pltpu
from jax.sharding import PartitionSpec as P

MESH = pl.DeviceIdType.MESH
LK = 64
TIME_STEP = 0.005
HOPPING_TIME = 0.5
FIELD_STEP = 0.0025
NX = 4
TILE = (8, 128)
IDENTITY = (1.0, 1.0, 0.0, 0.0, 1.0, 1.0, 0.0, 0.0, 0.0, 0.0)


def compose(late, early):
    l0, l11, l12, l21, l22, l3, lv0, lv1, lv2, lv3 = late
    e0, e11, e12, e21, e22, e3, ev0, ev1, ev2, ev3 = early
    return (
        l0 * e0,
        l11 * e11 + l12 * e21,
        l11 * e12 + l12 * e22,
        l21 * e11 + l22 * e21,
        l21 * e12 + l22 * e22,
        l3 * e3,
        l0 * ev0 + lv0,
        (l11 * ev1 + l12 * ev2) + lv1,
        (l21 * ev1 + l22 * ev2) + lv2,
        l3 * ev3 + lv3,
    )


def apply_map(parts, state):
    m0, a11, a12, a21, a22, m3, v0, v1, v2, v3 = parts
    s0, s1, s2, s3 = state
    return (
        m0 * s0 + v0,
        (a11 * s1 + a12 * s2) + v1,
        (a21 * s1 + a22 * s2) + v2,
        m3 * s3 + v3,
    )


def split(value):
    high = value.astype(jnp.bfloat16)
    low = (value - high.astype(jnp.float32)).astype(jnp.bfloat16)
    return high, low


def split_rows(value):
    high = value.astype(jnp.bfloat16).astype(jnp.float32)
    return jnp.concatenate([high, value - high], axis=0)


def halves(value):
    return jnp.concatenate([value[:, :128], value[:, 128:]], axis=0)


def far_first(count):
    def hops(step):
        return min(step, count - step)

    return sorted(range(1, count), key=lambda step: -hops(step))


def kernel(
    sizes,
    green,
    sigma,
    coupling,
    prev,
    init,
    rates,
    source,
    ids,
    t_step,
    lengths,
    prop_out,
    pp_out,
    hyb_out,
    g_vm,
    ghi,
    glo,
    sig_vm,
    coup_vm,
    prev_vm,
    src_vm,
    ids_vm,
    init_sm,
    rates_sm,
    t_sm,
    len_sm,
    a_buf,
    zr_buf,
    zi_buf,
    pr_buf,
    pi_buf,
    c_buf,
    c_rows,
    local_sem,
    send_sem,
    recv_sem,
    token_sem,
):
    n_mom, n_hist = sizes
    n_z = n_mom // 2
    n_y = n_hist // NX if n_hist >= NX else 1
    n_x = n_hist // n_y
    total = 128 * n_mom
    slots = 256 * n_hist
    mom, hist = lax.axis_index("mom"), lax.axis_index("hist")
    z, core = mom // 2, mom % 2
    y, x = hist // n_x, hist % n_x

    def hop(count, step):
        return min(step, count - step)

    hist_steps = sorted(
        [(dy, dx) for dy in range(n_y) for dx in range(n_x) if (dy, dx) != (0, 0)],
        key=lambda s: -(hop(n_y, s[0]) + hop(n_x, s[1])),
    )
    z_steps = far_first(n_z)

    def hist_peer(step):
        return (mom, ((y + step[0]) % n_y) * n_x + (x + step[1]) % n_x)

    def z_peer(step):
        return (((z + step) % n_z) * 2 + core, hist)

    partner = (z * 2 + 1 - core, hist)

    barrier = pltpu.get_barrier_semaphore()
    near = [hist_peer(step) for step in hist_steps] + [z_peer(1), z_peer(n_z - 1), partner]
    for peer in near:
        pl.semaphore_signal(barrier, inc=1, device_id=peer, device_id_type=MESH)
    small = [
        (sigma, sig_vm),
        (lengths, len_sm),
        (prev, prev_vm),
        (ids, ids_vm),
        (t_step, t_sm),
        (coupling, coup_vm),
        (source, src_vm),
        (rates, rates_sm),
        (init, init_sm),
    ]
    small_copies = [
        pltpu.make_async_copy(src, dst, local_sem.at[4 + i]) for i, (src, dst) in enumerate(small)
    ]
    green_copies = [
        pltpu.make_async_copy(green.at[r, b], g_vm.at[r, b], local_sem.at[2 * r + b])
        for r in range(2)
        for b in range(2)
    ]
    for copy in small_copies[:2]:
        copy.start()
    for copy in green_copies:
        copy.start()
    for copy in small_copies[2:]:
        copy.start()
    for copy in small_copies[:2]:
        copy.wait()

    length = len_sm[hist]
    lane256 = lax.broadcasted_iota(jnp.int32, (1, 256), 1)
    live256 = lane256 < length
    weight = jnp.where(live256, jnp.float32(TIME_STEP), jnp.float32(0.0))
    pad8 = jnp.zeros((8, 256), jnp.float32)
    left_sides = {}
    for b in range(2):
        re = [sig_vm[0, a, b : b + 1, :] * weight for a in range(2)]
        im = [sig_vm[1, a, b : b + 1, :] * weight for a in range(2)]
        for r, rows in ((0, re + im), (1, [-im[0], -im[1]] + re)):
            stacked = split_rows(jnp.concatenate(rows, axis=0))
            left_sides[r, b] = jnp.concatenate([stacked, pad8], axis=0).astype(jnp.bfloat16)
    acc = jnp.zeros((16, 256), jnp.float32)
    contract_last = (((1,), (1,)), ((), ()))
    for r in range(2):
        for b in range(2):
            green_copies[2 * r + b].wait()
            high, low = split(g_vm[r, b].reshape(256, 256))
            ghi[r, b] = high
            glo[r, b] = low
            for part in (high, low):
                acc += lax.dot_general(
                    left_sides[r, b], part, contract_last, preferred_element_type=jnp.float32
                )
    mem4 = acc[0:4] + acc[4:8]
    a_buf[hist] = halves(mem4)

    pl.semaphore_wait(barrier, len(near))

    def send(buf, slot, which, peer):
        pltpu.make_async_remote_copy(
            src_ref=buf.at[slot],
            dst_ref=buf.at[slot],
            send_sem=send_sem.at[which],
            recv_sem=recv_sem.at[which],
            device_id=peer,
            device_id_type=MESH,
        ).start()

    def arrived(sem, buf, which, count):
        part = buf.at[pl.ds(0, count)]
        pltpu.make_async_copy(part, part, sem.at[which]).wait()

    for step in hist_steps:
        send(a_buf, hist, 0, hist_peer(step))

    reach = 1
    token = 0
    while reach < n_z // 2:
        for peer in (z_peer(reach), z_peer(n_z - reach)):
            pl.semaphore_signal(token_sem.at[token], inc=1, device_id=peer, device_id_type=MESH)
        if 2 * reach < n_z // 2:
            pl.semaphore_wait(token_sem.at[token], 2)
        reach *= 2
        token += 1

    for copy in small_copies[2:]:
        copy.wait()

    row = lax.broadcasted_iota(jnp.int32, TILE, 0)
    lane = lax.broadcasted_iota(jnp.int32, TILE, 1)
    field = jnp.full((1, 128), t_sm[0], jnp.int32).astype(jnp.float32) * FIELD_STEP
    momentum = ids_vm[...].reshape(1, 128)
    along_x = 2.0 * math.pi * (momentum & (LK - 1)).astype(jnp.float32) / LK
    along_y = 2.0 * math.pi * (momentum >> 6).astype(jnp.float32) / (total // LK)
    energy = -2.0 * (jnp.cos(along_x - field) + jnp.cos(along_y - field))
    angle = HOPPING_TIME * energy
    cosine = jnp.broadcast_to(jnp.cos(angle), TILE)
    sine = jnp.broadcast_to(jnp.sin(angle), TILE)
    before = jnp.concatenate(
        [prev_vm[r, a, c : c + 1, :] for c in range(2) for r in range(2) for a in range(2)], axis=0
    )
    is_real = (row & 2) == 0

    live_scale = jnp.where(live256, jnp.float32(1.0 / total), jnp.float32(0.0))
    real_side, imag_side = [], []
    for b in range(2):
        cr = coup_vm[0, b] * live_scale
        ci = coup_vm[1, b] * live_scale
        real_side.append(jnp.concatenate([cr, cr, -ci, -ci], axis=0))
        imag_side.append(jnp.concatenate([ci, ci, cr, cr], axis=0))

    upper = row >= 4
    live = jnp.where(upper, lane + 128, lane) < length
    drives = halves(src_vm[...])
    drive_scale = jnp.where(live, jnp.float32(TIME_STEP), jnp.float32(0.0))

    def bring(value, index):
        return pltpu.roll(value, 8 - index, axis=0) if index else value

    drive = [bring(drives, n) * drive_scale for n in range(4)]
    retain = []
    for n in range(4):
        decay = jnp.exp(-(jnp.full(TILE, rates_sm[n], jnp.float32) / slots))
        retain.append(jnp.where(live, decay, jnp.float32(1.0)))

    arrived(recv_sem, a_buf, 0, n_hist - 1)
    memory = a_buf[0]
    for h in range(1, n_hist):
        memory = memory + a_buf[h]
    summed = before + memory
    swapped = jnp.where(is_real, pltpu.roll(summed, 6, axis=0), -pltpu.roll(summed, 2, axis=0))
    current = cosine * summed + sine * swapped
    for c in range(2):
        for r in range(2):
            for a in range(2):
                at = 4 * c + 2 * r + a
                prop_out[r, a, c : c + 1, :] = current[at : at + 1, :]

    straight = jnp.concatenate([current[0:4], current[4:8]], axis=1)
    turned = jnp.concatenate([straight[2:4], -straight[0:2]], axis=0)
    rows = []
    for side in (straight, turned):
        twice = jnp.concatenate([side[i // 2 : i // 2 + 1] for i in range(8)], axis=0)
        rows.append(split_rows(twice).astype(jnp.bfloat16))
    contract_first = (((1,), (0,)), ((), ()))
    real_sum, imag_sum = None, None
    for b in range(2):
        out = jnp.zeros((16, 256), jnp.float32)
        for r in range(2):
            for part in (ghi, glo):
                out += lax.dot_general(
                    rows[r], part[r, b], contract_first, preferred_element_type=jnp.float32
                )
        both = out[0:8] + out[8:16]
        re, im = both * real_side[b], both * imag_side[b]
        real_sum = re if b == 0 else real_sum + re
        imag_sum = im if b == 0 else imag_sum + im

    def fold(value):
        first, second = value[:, :128], value[:, 128:]
        first = first + pltpu.roll(first, 4, axis=0)
        second = second + pltpu.roll(second, 4, axis=0)
        return jnp.where(upper, second, first)

    zr_buf[z] = fold(real_sum)
    zi_buf[z] = fold(imag_sum)
    if token:
        pl.semaphore_wait(token_sem.at[token - 1], 2)
    for step in z_steps:
        send(zr_buf, z, 1, z_peer(step))
    for step in z_steps:
        send(zi_buf, z, 2, z_peer(step))

    def total_over_z(buf, which):
        arrived(recv_sem, buf, which, n_z - 1)
        value = buf[0]
        for i in range(1, n_z):
            value = value + buf[i]
        return value

    pr_buf[core] = total_over_z(zr_buf, 1)
    send(pr_buf, core, 3, partner)
    arrived(recv_sem, pr_buf, 3, 1)
    delta_re = pr_buf[0] + pr_buf[1]

    d00, d01, d10, d11 = (TIME_STEP * bring(delta_re, i) for i in range(4))
    maps = (
        retain[0],
        retain[1] - d00,
        -d01,
        -d10,
        retain[2] - d11,
        retain[3] - (d00 + d11),
        *drive,
    )
    shift = 1
    while shift < 128:
        inside = lane >= shift
        early = tuple(
            jnp.where(inside, pltpu.roll(part, shift, axis=1), jnp.float32(one))
            for part, one in zip(maps, IDENTITY)
        )
        maps = compose(maps, early)
        shift *= 2
    ends = tuple(jnp.broadcast_to(part[:, 127:128], TILE) for part in maps)
    first_half = tuple(pltpu.roll(part, 4, axis=0) for part in ends)
    block = compose(ends, first_half)
    packed = jnp.zeros(TILE, jnp.float32)
    for i, part in enumerate(block):
        packed = jnp.where(lane == i, part, packed)
    c_buf[hist] = packed[4:5, :]
    for step in hist_steps:
        send(c_buf, hist, 5, hist_peer(step))

    prefix = compose(
        maps,
        tuple(
            jnp.where(upper, part, jnp.float32(one)) for part, one in zip(first_half, IDENTITY)
        ),
    )
    pi_buf[core] = total_over_z(zi_buf, 2)
    send(pi_buf, core, 4, partner)

    arrived(recv_sem, c_buf, 5, n_hist - 1)
    gathered = c_buf[...].reshape(n_hist, 128)
    for i in range(10):
        c_rows[i] = jnp.broadcast_to(gathered[:, i : i + 1], (n_hist, 128))
    state = tuple(jnp.full((1, 128), init_sm[n], jnp.float32) for n in range(4))
    start = state
    for j in range(n_hist):
        state = apply_map(tuple(c_rows[i, j : j + 1, :] for i in range(10)), state)
        if j + 1 < n_hist:
            mine = hist == j + 1
            start = tuple(jnp.where(mine, new, old) for new, old in zip(state, start))
    states = apply_map(prefix, tuple(jnp.broadcast_to(part, TILE) for part in start))
    for n in range(4):
        pp_out[n : n + 1, 0:128] = states[n][0:1]
        pp_out[n : n + 1, 128:256] = states[n][4:5]
    norm = state[0] * state[0] + state[1] * state[1] + state[2] * state[2] + state[3] * state[3]
    scale = jnp.broadcast_to(1.0 / jnp.sqrt(1.0 + norm), TILE)
    arrived(recv_sem, pi_buf, 4, 1)
    delta_im = pi_buf[0] + pi_buf[1]
    for r, delta in ((0, delta_re), (1, delta_im)):
        scaled = delta * scale
        for a in range(2):
            for half in range(2):
                hyb_out[r, a, :, half * 128 : half * 128 + 128] = scaled[
                    half * 4 + 2 * a : half * 4 + 2 * a + 2
                ]

    for buf, which, count in (
        (a_buf, 0, n_hist - 1),
        (zr_buf, 1, n_z - 1),
        (zi_buf, 2, n_z - 1),
        (pr_buf, 3, 1),
        (pi_buf, 4, 1),
        (c_buf, 5, n_hist - 1),
    ):
        arrived(send_sem, buf, which, count)


def on_device(sizes, *args):
    f32 = jnp.float32
    n_mom, n_hist = sizes
    n_z = n_mom // 2
    hbm = pl.BlockSpec(memory_space=pl.ANY)
    vmem = pl.BlockSpec(memory_space=pltpu.VMEM)
    return pl.pallas_call(
        functools.partial(kernel, sizes),
        out_shape=(
            jax.ShapeDtypeStruct((2, 2, 2, 128), f32),
            jax.ShapeDtypeStruct((4, 256), f32),
            jax.ShapeDtypeStruct((2, 2, 2, 256), f32),
        ),
        in_specs=[hbm] * 10,
        out_specs=(vmem, vmem, vmem),
        scratch_shapes=[
            pltpu.VMEM((2, 2, 2, 128, 256), f32),
            pltpu.VMEM((2, 2, 256, 256), jnp.bfloat16),
            pltpu.VMEM((2, 2, 256, 256), jnp.bfloat16),
            pltpu.VMEM((2, 2, 2, 256), f32),
            pltpu.VMEM((2, 2, 2, 256), f32),
            pltpu.VMEM((2, 2, 2, 128), f32),
            pltpu.VMEM((4, 256), f32),
            pltpu.VMEM((128,), jnp.int32),
            pltpu.SMEM((4,), f32),
            pltpu.SMEM((4,), f32),
            pltpu.SMEM((1,), jnp.int32),
            pltpu.SMEM((n_hist,), jnp.int32),
            pltpu.VMEM((n_hist, 8, 128), f32),
            pltpu.VMEM((n_z, 8, 128), f32),
            pltpu.VMEM((n_z, 8, 128), f32),
            pltpu.VMEM((2, 8, 128), f32),
            pltpu.VMEM((2, 8, 128), f32),
            pltpu.VMEM((n_hist, 1, 128), f32),
            pltpu.VMEM((10, n_hist, 128), f32),
            pltpu.SemaphoreType.DMA((13,)),
            pltpu.SemaphoreType.DMA((6,)),
            pltpu.SemaphoreType.DMA((6,)),
            pltpu.SemaphoreType.REGULAR((4,)),
        ],
        compiler_params=pltpu.CompilerParams(collective_id=0, has_side_effects=True),
        name="dmft_step",
    )(*args)


def solution(mesh):
    sizes = (mesh.shape["mom"], mesh.shape["hist"])
    placed = (
        P(None, None, None, "mom", "hist"),
        P(None, None, None, "hist"),
        P(None, None, None, "hist"),
        P(None, None, None, "mom"),
        P(),
        P(),
        P(None, "hist"),
        P("mom"),
        P(),
        P(),
    )
    return jax.shard_map(
        functools.partial(on_device, sizes),
        mesh=mesh,
        in_specs=placed,
        out_specs=(P(None, None, None, "mom"), P(None, "hist"), P(None, None, None, "hist")),
        check_vma=False,
    )
```

time: 227 us -> 38.6 us (0.17)
  the two profiles are of different devices: /device:TPU:2 before, /device:TPU:1 now
where the time goes in v1:
time: 38.6 us; the launch traced here: 38.4 us
  Pallas kernels  34.6 us (90%)
  local copies, waits for them, and re-layouts  2.45 us (6%)
  between operations  1.31 us (3%)
    pallas_call x1, Pallas kernels, on_device(): pl.pallas_call(functools.partial(kernel, sizes), out_shape=(jax.ShapeDtyp...  34.6 us
    unnamed x9, local copies, waits for them, and re-layouts  2.45 us

profile of v1, /device:TPU:1, one launch (start us, length us, event | category | flops | bytes accessed | tf_op | source)
XLA Modules:
  0.0 38.4 jit_solution(2867802481386373762)
XLA Ops:
  1.3 34.6 %dmft_step.1 = (f32[2,2,2,128]{3,2,1,0:T(2,128)}, f32[4,256]{1,0:T(4,128)}, f32[2,2,2,256]{3,2,1,0:T(2,128)}) custom-call(f32[2,2,2,128,256]{4,3,2,1,0:T(8,128)} %green.1, f32[2,2,2,256]{3,2,1,0:T(2,128)} %sigma.1, f32[2,2,2,256]{3,2,1,0:T(2,128)} %coupling.1, f32[2,2,2,128]{3,2,1,0:T(2,128)} %prev.1, f32[4]{0:T(128)} %init.1, f32[4]{0:T(128)} %rates.1, ...), custom_call_target="tpu_custom_call" | custom-call | tf_op jit(solution)/shard_map/dmft_step/pallas_call | solution.py:408
  35.9 0.0 copy-start.2
  35.9 0.0 copy-start.1
  35.9 0.7 %copy-done.2 = f32[2,2,2,128]{3,2,1,0:T(2,128)S(1)} copy-done((f32[2,2,2,128]{3,2,1,0:T(2,128)S(1)}, f32[2,2,2,128]{3,2,1,0:T(2,128)}, u32[]{:S(2)}) %copy-start.2) | copy-done | bytes 4120
  36.6 0.0 copy-start
  36.6 0.6 %copy.17 = f32[2,2,2,128]{3,2,1,0:T(2,128)} copy(f32[2,2,2,128]{3,2,1,0:T(2,128)S(1)} %copy-done.2) | data formatting | bytes 8192
  37.2 0.0 copy-done.1
  37.2 0.6 %copy.18 = f32[4,256]{1,0:T(4,128)} copy(f32[4,256]{1,0:T(4,128)S(1)} %copy-done.1) | data formatting | bytes 8192
  37.8 0.0 copy-done
  37.8 0.6 %copy.19 = f32[2,2,2,256]{3,2,1,0:T(2,128)} copy(f32[2,2,2,256]{3,2,1,0:T(2,128)S(1)} %copy-done) | data formatting | bytes 16384
Async XLA Ops:
  35.9 0.7 %copy-start.2 = (f32[2,2,2,128]{3,2,1,0:T(2,128)S(1)}, f32[2,2,2,128]{3,2,1,0:T(2,128)}, u32[]{:S(2)}) copy-start(f32[2,2,2,128]{3,2,1,0:T(2,128)} %get-tuple-element.6) | copy-start | bytes 12292
  35.9 1.3 %copy-start.1 = (f32[4,256]{1,0:T(4,128)S(1)}, f32[4,256]{1,0:T(4,128)}, u32[]{:S(2)}) copy-start(f32[4,256]{1,0:T(4,128)} %get-tuple-element.7) | copy-start | bytes 12292
  36.6 1.2 %copy-start = (f32[2,2,2,256]{3,2,1,0:T(2,128)S(1)}, f32[2,2,2,256]{3,2,1,0:T(2,128)}, u32[]{:S(2)}) copy-start(f32[2,2,2,256]{3,2,1,0:T(2,128)} %get-tuple-element.8) | copy-start | bytes 24580

commit v2 on v1

--- a/solution.py
+++ b/solution.py
@@ -136,7 +136,11 @@
     partner = (z * 2 + 1 - core, hist)
 
     barrier = pltpu.get_barrier_semaphore()
-    near = [hist_peer(step) for step in hist_steps] + [z_peer(1), z_peer(n_z - 1), partner]
+    reach = n_z // 4
+    near_z = sorted({step % n_z for r in range(1, reach + 1) for step in (r, -r)})
+    near = [hist_peer(step) for step in hist_steps] + [z_peer(step) for step in near_z]
+    near.append(partner)
+    far_z = (z_peer(reach), z_peer(n_z - reach))
     for peer in near:
         pl.semaphore_signal(barrier, inc=1, device_id=peer, device_id_type=MESH)
     small = [
@@ -164,6 +168,7 @@
         copy.start()
     for copy in small_copies[2:]:
         copy.start()
+
     for copy in small_copies[:2]:
         copy.wait()
 
@@ -195,6 +200,8 @@
     a_buf[hist] = halves(mem4)
 
     pl.semaphore_wait(barrier, len(near))
+    for peer in far_z:
+        pl.semaphore_signal(token_sem.at[0], inc=1, device_id=peer, device_id_type=MESH)
 
     def send(buf, slot, which, peer):
         pltpu.make_async_remote_copy(
@@ -213,22 +220,12 @@
     for step in hist_steps:
         send(a_buf, hist, 0, hist_peer(step))
 
-    reach = 1
-    token = 0
-    while reach < n_z // 2:
-        for peer in (z_peer(reach), z_peer(n_z - reach)):
-            pl.semaphore_signal(token_sem.at[token], inc=1, device_id=peer, device_id_type=MESH)
-        if 2 * reach < n_z // 2:
-            pl.semaphore_wait(token_sem.at[token], 2)
-        reach *= 2
-        token += 1
-
     for copy in small_copies[2:]:
         copy.wait()
 
     row = lax.broadcasted_iota(jnp.int32, TILE, 0)
     lane = lax.broadcasted_iota(jnp.int32, TILE, 1)
-    field = jnp.full((1, 128), t_sm[0], jnp.int32).astype(jnp.float32) * FIELD_STEP
+    field = jnp.full((1, 128), t_sm[0, 0], jnp.int32).astype(jnp.float32) * FIELD_STEP
     momentum = ids_vm[...].reshape(1, 128)
     along_x = 2.0 * math.pi * (momentum & (LK - 1)).astype(jnp.float32) / LK
     along_y = 2.0 * math.pi * (momentum >> 6).astype(jnp.float32) / (total // LK)
@@ -303,11 +300,13 @@
         return jnp.where(upper, second, first)
 
     zr_buf[z] = fold(real_sum)
-    zi_buf[z] = fold(imag_sum)
-    if token:
-        pl.semaphore_wait(token_sem.at[token - 1], 2)
+    pl.semaphore_wait(token_sem.at[0], 2)
     for step in z_steps:
         send(zr_buf, z, 1, z_peer(step))
+    pi_buf[core] = fold(imag_sum)
+    send(pi_buf, core, 4, partner)
+    arrived(recv_sem, pi_buf, 4, 1)
+    zi_buf[z] = pi_buf[0] + pi_buf[1]
     for step in z_steps:
         send(zi_buf, z, 2, z_peer(step))
 
@@ -358,9 +357,6 @@
             jnp.where(upper, part, jnp.float32(one)) for part, one in zip(first_half, IDENTITY)
         ),
     )
-    pi_buf[core] = total_over_z(zi_buf, 2)
-    send(pi_buf, core, 4, partner)
-
     arrived(recv_sem, c_buf, 5, n_hist - 1)
     gathered = c_buf[...].reshape(n_hist, 128)
     for i in range(10):
@@ -378,8 +374,7 @@
         pp_out[n : n + 1, 128:256] = states[n][4:5]
     norm = state[0] * state[0] + state[1] * state[1] + state[2] * state[2] + state[3] * state[3]
     scale = jnp.broadcast_to(1.0 / jnp.sqrt(1.0 + norm), TILE)
-    arrived(recv_sem, pi_buf, 4, 1)
-    delta_im = pi_buf[0] + pi_buf[1]
+    delta_im = total_over_z(zi_buf, 2)
     for r, delta in ((0, delta_re), (1, delta_im)):
         scaled = delta * scale
         for a in range(2):
@@ -399,19 +394,25 @@
         arrived(send_sem, buf, which, count)
 
 
+def put_out(*refs):
+    sem = refs[6]
+    copies = [pltpu.make_async_copy(refs[i], refs[3 + i], sem.at[i]) for i in range(3)]
+    for copy in copies:
+        copy.start()
+    for copy in copies:
+        copy.wait()
+
+
 def on_device(sizes, *args):
     f32 = jnp.float32
     n_mom, n_hist = sizes
     n_z = n_mom // 2
-    hbm = pl.BlockSpec(memory_space=pl.ANY)
+    shapes = ((2, 2, 2, 128), (4, 256), (2, 2, 2, 256))
+    hbm = pl.BlockSpec(memory_space=pltpu.HBM)
     vmem = pl.BlockSpec(memory_space=pltpu.VMEM)
-    return pl.pallas_call(
+    results = pl.pallas_call(
         functools.partial(kernel, sizes),
-        out_shape=(
-            jax.ShapeDtypeStruct((2, 2, 2, 128), f32),
-            jax.ShapeDtypeStruct((4, 256), f32),
-            jax.ShapeDtypeStruct((2, 2, 2, 256), f32),
-        ),
+        out_shape=tuple(pltpu.VMEM(shape, f32) for shape in shapes),
         in_specs=[hbm] * 10,
         out_specs=(vmem, vmem, vmem),
         scratch_shapes=[
@@ -425,7 +426,7 @@
             pltpu.VMEM((128,), jnp.int32),
             pltpu.SMEM((4,), f32),
             pltpu.SMEM((4,), f32),
-            pltpu.SMEM((1,), jnp.int32),
+            pltpu.SMEM((1, 1), jnp.int32),
             pltpu.SMEM((n_hist,), jnp.int32),
             pltpu.VMEM((n_hist, 8, 128), f32),
             pltpu.VMEM((n_z, 8, 128), f32),
@@ -437,11 +438,19 @@
             pltpu.SemaphoreType.DMA((13,)),
             pltpu.SemaphoreType.DMA((6,)),
             pltpu.SemaphoreType.DMA((6,)),
-            pltpu.SemaphoreType.REGULAR((4,)),
+            pltpu.SemaphoreType.REGULAR((1,)),
         ],
         compiler_params=pltpu.CompilerParams(collective_id=0, has_side_effects=True),
         name="dmft_step",
-    )(*args)
+    )(*args[:8], args[8].reshape(1, 1), args[9])
+    return pl.pallas_call(
+        put_out,
+        out_shape=tuple(jax.ShapeDtypeStruct(shape, f32) for shape in shapes),
+        in_specs=[vmem] * 3,
+        out_specs=(hbm,) * 3,
+        scratch_shapes=[pltpu.SemaphoreType.DMA((3,))],
+        name="put_out",
+    )(*(pltpu.with_memory_space_constraint(part, pltpu.VMEM) for part in results))
 
 
 def solution(mesh):

time: 38.6 us -> 35.8 us (0.927)
  local copies, waits for them, and re-layouts: 2.45 us -> 0 us
    unnamed x9 -> x0, local copies, waits for them, and re-layouts: 2.45 us -> none
    pallas_call x1 -> x2, Pallas kernels: 34.6 us -> 34.4 us  [the longest x1 33.7 us: on_device(): pl.pallas_call(functools.partial(kernel, sizes), out_shape=tuple((pltpu.V...]
where the time goes in v2:
time: 35.8 us; the launch traced here: 35.6 us
  Pallas kernels  34.4 us (96%)
  between operations  1.29 us (4%)
    pallas_call x1, Pallas kernels, on_device(): pl.pallas_call(functools.partial(kernel, sizes), out_shape=tuple((pltpu.V...  33.7 us

profile of v2, /device:TPU:1, one launch (start us, length us, event | category | flops | bytes accessed | tf_op | source)
XLA Modules:
  0.0 35.6 jit_solution(18431493452660710362)
XLA Ops:
  1.3 33.7 %dmft_step.1 = (f32[2,2,2,128]{3,2,1,0:T(2,128)S(1)}, f32[4,256]{1,0:T(4,128)S(1)}, f32[2,2,2,256]{3,2,1,0:T(2,128)S(1)}) custom-call(f32[2,2,2,128,256]{4,3,2,1,0:T(8,128)} %green.1, f32[2,2,2,256]{3,2,1,0:T(2,128)} %sigma.1, f32[2,2,2,256]{3,2,1,0:T(2,128)} %coupling.1, f32[2,2,2,128]{3,2,1,0:T(2,128)} %prev.1, f32[4]{0:T(128)} %init.1, f32[4]{0:T(128)} %rates.1, ...), custom_call_target="tpu_custom_call" | custom-call | tf_op jit(solution)/shard_map/dmft_step/pallas_call | solution.py:413
  35.0 0.6 %put_out.1 = (f32[2,2,2,128]{3,2,1,0:T(2,128)}, f32[4,256]{1,0:T(4,128)}, f32[2,2,2,256]{3,2,1,0:T(2,128)}) custom-call(f32[2,2,2,128]{3,2,1,0:T(2,128)S(1)} %get-tuple-element.6.refs_0_, f32[4,256]{1,0:T(4,128)S(1)} %get-tuple-element.7.refs_1_, f32[2,2,2,256]{3,2,1,0:T(2,128)S(1)} %get-tuple-element.8.refs_2_), custom_call_target="tpu_custom_call" | custom-call | tf_op jit(solution)/shard_map/put_out/pallas_call | solution.py:446
